TPU v7x, 128 devices: a whole 4x4x4 slice. The times are simulated.
128 devices in a mesh: blk: 8 (over x_lo, y), head: 8 (over z, core), grp: 2 (over x_hi).
Axes of the slice: x: 4 (x_hi: 2, x_lo: 2; x = x_hi * 2 + x_lo), y: 4, z: 4, core: 2. Of those that a mesh axis runs over, the one named last changes fastest.
Arguments:
- t_query: bfloat16 [8192, 4096], P('blk', ('head', 'grp')), may hold values from -80 to 80
- t_key: bfloat16 [8192, 4096], P('blk', ('head', 'grp')), may hold values from -80 to 80
- t_value: bfloat16 [8192, 4096], P('blk', ('head', 'grp')), may hold values from -6 to 6
- t_out: bfloat16 [4096, 4096], P(('head', 'grp')), may hold values from -0.09375 to 0.09375
- s_query: bfloat16 [8192, 2048], P('blk', ('head', 'grp')), may hold values from -80 to 80
- s_key: bfloat16 [8192, 2048], P('blk', ('head', 'grp')), may hold values from -80 to 80
- s_value: bfloat16 [8192, 2048], P('blk', ('head', 'grp')), may hold values from -6 to 6
- s_out: bfloat16 [2048, 4096], P(('head', 'grp')), may hold values from -0.125 to 0.125
- segments: int32 [8192], P('blk'), may hold values from 0 to 1, never falling along the last dimension, each value on 1 to 8128 neighbouring positions
- selection: int32 [128, 16], P('blk'), may hold values from 0 to 127, as said below
Outputs:
- mismatch: float32 [8192, 4096], P('blk', ('head', 'grp'))
- s_dq: float32 [8192, 2048], P('blk', ('head', 'grp'))
- s_dk: float32 [8192, 2048], P('blk', ('head', 'grp'))
- s_dv: float32 [8192, 2048], P('blk', ('head', 'grp'))
Inputs may be any that keep to these rules, and one draw needn't show every extreme that they name: `selection`: entry 0 of row b is b itself; for b >= 64, entry 1 of row b is b - 64; every entry of row b lies between 0 and b; entries of a row may repeat. `segments`: document numbers never fall along the sequence.
All inputs are finite; a program needn't handle non-finite values.
Results may differ from a plain program's by a relative error of at most 0.015.
Values may be sent and summed in bfloat16 or wider, within the bound.
No kernel may reach another device: no remote copies, remote signals or barrier semaphores. Data moves between devices by JAX's collectives and lax.ppermute only.
A program may use at most 128 MiB of HBM per device.

v0:
```python
import math
import jax
import jax.numpy as jnp
from jax import lax
from jax.sharding import PartitionSpec as P

HD = 128
BS = 64
NSEL = 16
masked_score = -1e30


def student_forward(queries, key_all, value_all, segment_all, selection, first_row):
    row_count = queries.shape[0]
    head_count = queries.shape[1] // HD
    blocks = row_count // BS
    query_blocks = queries.reshape(blocks, BS, head_count, HD)
    key_blocks = key_all.reshape(-1, BS, head_count, HD)[selection].reshape(
        blocks, NSEL * BS, head_count, HD
    )
    value_blocks = value_all.reshape(-1, BS, head_count, HD)[selection].reshape(
        blocks, NSEL * BS, head_count, HD
    )
    key_pos = (selection[:, :, None] * BS + jnp.arange(BS)[None, None, :]).reshape(
        blocks, NSEL * BS
    )
    query_pos = (first_row + jnp.arange(row_count)).reshape(blocks, BS)
    key_seg = segment_all[key_pos]
    query_seg = segment_all[query_pos]
    scores = jnp.einsum(
        "bqhd,bkhd->bhqk", query_blocks, key_blocks, preferred_element_type=jnp.float32
    ) * HD ** (-0.5)
    allowed = (
        (key_pos[:, None, :] <= query_pos[:, :, None])
        & (key_seg[:, None, :] == query_seg[:, :, None])
    )[:, None]
    scores = jnp.where(allowed, scores, masked_score)
    largest = jnp.max(scores, axis=3, keepdims=True)
    weights = jnp.where(allowed, jnp.exp(scores - largest), 0.0)
    weights = weights / jnp.sum(weights, axis=3, keepdims=True)
    value_wide = value_blocks.astype(jnp.float32)
    blended = jnp.einsum("bhqk,bkhd->bqhd", weights, value_wide, precision=lax.Precision.HIGHEST)
    saved = (query_blocks, key_blocks, value_wide, weights, blended)
    return (blended.reshape(row_count, head_count * HD), saved)


def student_backward(grad_attn, saved, selection, token_count):
    query_blocks, key_blocks, value_wide, weights, blended = saved
    blocks, _, head_count, _ = query_blocks.shape
    row_count = blocks * BS
    grad_blocks = grad_attn.reshape(blocks, BS, head_count, HD)
    value_grad = jnp.einsum(
        "bhqk,bqhd->bkhd", weights, grad_blocks, precision=lax.Precision.HIGHEST
    )
    weight_grad = jnp.einsum(
        "bqhd,bkhd->bhqk", grad_blocks, value_wide, precision=lax.Precision.HIGHEST
    )
    row_dots = jnp.sum(grad_blocks * blended, axis=3).transpose(0, 2, 1)[..., None]
    score_grad = weights * (weight_grad - row_dots) * HD ** (-0.5)
    query_grad = jnp.einsum(
        "bhqk,bkhd->bqhd",
        score_grad,
        key_blocks.astype(jnp.float32),
        precision=lax.Precision.HIGHEST,
    )
    key_grad = jnp.einsum(
        "bhqk,bqhd->bkhd",
        score_grad,
        query_blocks.astype(jnp.float32),
        precision=lax.Precision.HIGHEST,
    )
    flat_sel = selection.reshape(-1)
    width = head_count * HD
    key_total = (
        jnp.zeros((token_count // BS, BS, width), jnp.float32)
        .at[flat_sel]
        .add(key_grad.reshape(blocks * NSEL, BS, width))
    )
    value_total = (
        jnp.zeros((token_count // BS, BS, width), jnp.float32)
        .at[flat_sel]
        .add(value_grad.reshape(blocks * NSEL, BS, width))
    )
    return (
        query_grad.reshape(row_count, width),
        key_total.reshape(token_count, width),
        value_total.reshape(token_count, width),
    )


def teacher_update(
    carried, key_rows, value_rows, seg_rows, first_key, queries, query_seg, query_pos
):
    running_max, running_sum, weighted = carried
    head_count = queries.shape[1]
    key_heads = key_rows.reshape(key_rows.shape[0], head_count, HD)
    value_heads = value_rows.reshape(value_rows.shape[0], head_count, HD)
    scores = jnp.einsum(
        "qhd,khd->hqk", queries, key_heads, preferred_element_type=jnp.float32
    ) * HD ** (-0.5)
    key_pos = first_key + jnp.arange(key_rows.shape[0])
    allowed = (
        (key_pos[None, :] <= query_pos[:, None]) & (seg_rows[None, :] == query_seg[:, None])
    )[None]
    scores = jnp.where(allowed, scores, masked_score)
    new_max = jnp.maximum(running_max, jnp.max(scores, axis=2))
    factor = jnp.exp(running_max - new_max)
    weights = jnp.where(allowed, jnp.exp(scores - new_max[..., None]), 0.0)
    running_sum = factor * running_sum + jnp.sum(weights, axis=2)
    product = jnp.einsum(
        "hqk,khd->hqd",
        weights.astype(jnp.bfloat16),
        value_heads,
        preferred_element_type=jnp.float32,
    )
    weighted = factor[..., None] * weighted + product
    return (new_max, running_sum, weighted)


def teacher_fold(carried, key_rows, value_rows, seg_rows, queries, query_seg, query_pos):
    piece_rows = key_rows.shape[0]
    block_rows = math.gcd(piece_rows, 512)
    turn_count = piece_rows // block_rows
    last_query = query_pos[-1]

    def one_turn(turn_index, status):
        offset = turn_index * block_rows
        key_block = lax.dynamic_slice_in_dim(key_rows, offset, block_rows, 0)
        value_block = lax.dynamic_slice_in_dim(value_rows, offset, block_rows, 0)
        seg_block = lax.dynamic_slice_in_dim(seg_rows, offset, block_rows, 0)

        def compute(inner):
            return teacher_update(
                inner, key_block, value_block, seg_block, offset, queries, query_seg, query_pos
            )

        def keep(inner):
            return inner

        return lax.cond(offset > last_query, keep, compute, status)

    return lax.fori_loop(0, turn_count, one_turn, carried)


def on_device(t_query, t_key, t_value, t_out, s_query, s_key, s_value, s_out, segments, selection):
    row_count = t_query.shape[0]
    head_count = t_query.shape[1] // HD
    cycle_size = lax.axis_size("blk")
    my_index = lax.axis_index("blk")
    first_row = my_index * row_count
    token_count = row_count * cycle_size
    query_pos = first_row + jnp.arange(row_count)
    queries = t_query.reshape(row_count, head_count, HD)
    initial = (
        jnp.full((head_count, row_count), masked_score, jnp.float32),
        jnp.zeros((head_count, row_count), jnp.float32),
        jnp.zeros((head_count, row_count, HD), jnp.float32),
    )
    teacher_state = teacher_fold(
        initial,
        lax.all_gather(t_key, "blk", axis=0, tiled=True),
        lax.all_gather(t_value, "blk", axis=0, tiled=True),
        lax.all_gather(segments, "blk", axis=0, tiled=True),
        queries,
        segments,
        query_pos,
    )
    key_full, value_full, seg_full = (
        lax.all_gather(s_key, "blk", axis=0, tiled=True),
        lax.all_gather(s_value, "blk", axis=0, tiled=True),
        lax.all_gather(segments, "blk", axis=0, tiled=True),
    )
    t_attn = (
        (teacher_state[2] / teacher_state[1][..., None])
        .transpose(1, 0, 2)
        .reshape(row_count, head_count * HD)
    )
    t_attn = t_attn.astype(jnp.bfloat16)
    student_full, saved = student_forward(
        s_query, key_full, value_full, seg_full, selection, first_row
    )
    s_attn = student_full.astype(jnp.bfloat16)
    partial_terms = jnp.dot(s_attn, s_out, preferred_element_type=jnp.float32) - jnp.dot(
        t_attn, t_out, preferred_element_type=jnp.float32
    )
    contract = (((1,), (1,)), ((), ()))
    mismatch = lax.psum_scatter(
        partial_terms.astype(jnp.bfloat16), ("head", "grp"), scatter_dimension=1, tiled=True
    ).astype(jnp.float32)
    grad_attn = lax.dot_general(
        lax.all_gather(mismatch.astype(jnp.bfloat16), ("head", "grp"), axis=1, tiled=True),
        s_out,
        contract,
        preferred_element_type=jnp.float32,
    )
    grad_query, grad_keys, grad_values = student_backward(grad_attn, saved, selection, token_count)
    key_grads, value_grads = (
        lax.psum_scatter(
            grad_keys.astype(jnp.bfloat16), "blk", scatter_dimension=0, tiled=True
        ).astype(jnp.float32),
        lax.psum_scatter(
            grad_values.astype(jnp.bfloat16), "blk", scatter_dimension=0, tiled=True
        ).astype(jnp.float32),
    )
    return (mismatch, grad_query, key_grads, value_grads)


def solution(mesh):
    in_specs = (
        P("blk", ("head", "grp")),
        P("blk", ("head", "grp")),
        P("blk", ("head", "grp")),
        P(("head", "grp"), None),
        P("blk", ("head", "grp")),
        P("blk", ("head", "grp")),
        P("blk", ("head", "grp")),
        P(("head", "grp"), None),
        P("blk"),
        P("blk", None),
    )
    out_specs = (
        P("blk", ("head", "grp")),
        P("blk", ("head", "grp")),
        P("blk", ("head", "grp")),
        P("blk", ("head", "grp")),
    )
    return jax.shard_map(
        on_device, mesh=mesh, in_specs=in_specs, out_specs=out_specs, check_vma=False
    )
```

profile of v0, /device:TPU:0, one launch (start us, length us, event | category | flops | bytes accessed | tf_op | source)
XLA Modules:
  0.0 699.5 jit_solution(14955056844412528402)
XLA Ops:
  7.2 0.7 all-gather.6.cloned.1.call-update
  8.0 0.7 all-gather.8.cloned.1.call-update
  8.7 2.0 copy.27
  10.8 2.0 copy.29
  13.0 0.7 broadcast_multiply_fusion
  13.7 0.1 add.182
  13.8 0.1 add.190
  13.9 0.1 add.183
  14.0 0.1 reshape.321
  14.1 28.7 %all_gather.20 = s32[8192]{0:T(1024)S(1)} all-gather(s32[1024]{0:T(1024)S(1)} %copy-done.12), channel_id=1, replica_groups=mesh['blk'=8,'head'=8,'grp'=2] {'blk'}, dimensions={0}, use_global_device_ids=true | all-gather | bytes 36864 | tf_op jit(solution)/shard_map/all_gather | solution.py:171
  42.8 6.1 gather_fusion.2
  49.2 90.5 %gather_fusion.1 = s32[16384]{0:T(1024)S(1)} fusion(s32[8192]{0:T(1024)S(1)} %all_gather.20, s32[16384]{0:T(1024)S(1)} %broadcast_clamp_fusion), kind=kCustom, calls=%fused_computation.1 | custom fusion | bytes 196608 | tf_op jit(solution)/shard_map/gather | solution.py:28
  139.8 0.6 slice.3
  140.4 0.2 copy.28
  140.6 0.3 copy.30
  141.0 4.8 gather_fusion
  145.8 4.7 gather_fusion.3
  150.5 6.2 fusion.27
  156.7 6.7 fusion.28
  163.3 8.1 %fusion.29 = f32[1024,4096]{1,0:T(8,128)} fusion(bf16[1024,128]{1,0:T(8,128)(2,1)S(1)} %bitcast.102, bf16[128,4096]{1,0:T(8,128)(2,1)S(1)} %copy-done.7), kind=kOutput, calls=%fused_computation.60 | convolution fusion | flops 1073741824 | bytes 18087936 | tf_op jit(solution)/shard_map/dot_general | solution.py:183
  171.4 32.4 %all-gather.12.cloned.1.call-done = bf16[8192,256]{0,1:T(8,128)(2,1)} async-done(((bf16[1024,256]{0,1:T(8,128)(2,1)}), bf16[8192,256]{0,1:T(8,128)(2,1)}) %all-gather.12.cloned.1.call-update) | async-done | bytes 4194320 | tf_op jit(solution)/shard_map/all_gather | solution.py:162
  203.9 1.0 broadcast_in_dim.72
  204.9 25.1 %while.18 = (s32[]{:T(128)}, f32[2,1024]{1,0:T(2,128)S(1)}, f32[2,1024]{1,0:T(2,128)S(1)}, f32[2,1024,128]{2,1,0:T(8,128)}, s32[]{:T(128)}, /*index=5*/s32[8192]...) while((s32[]{:T(128)}, f32[2,1024]{1,0:T(2,128)S(1)}, ...), condition=%wide.region_7.8_spmd.clone, body=%wide.region_2.7_spmd.clone.sunk | while | flops 552605184 | bytes 27425168 | solution.py:142
  205.5 7.0 conditional.3
  205.6 0.1 dynamic_slice.34
  205.7 0.5 compare_and_fusion
  206.2 1.1 constant_dynamic-slice_fusion
  207.2 1.1 fusion.2
  208.4 1.1 fusion.4
  209.5 2.0 fusion.8
  211.5 1.0 copy-done.5
  213.1 7.0 conditional.3
  213.2 0.1 dynamic_slice.34
  213.3 0.5 compare_and_fusion
  213.8 1.1 constant_dynamic-slice_fusion
  214.8 1.1 fusion.2
  216.0 1.1 fusion.4
  217.1 2.0 fusion.8
  219.1 1.0 copy-done.5
  230.0 1.6 copy.31
  231.6 0.1 divide_convert_fusion
  231.7 11.4 %subtract_convert_fusion = bf16[1024,4096]{1,0:T(8,128)(2,1)} fusion(f32[1024,4096]{1,0:T(8,128)} %fusion.29, bf16[1024,256]{0,1:T(8,128)(2,1)S(1)} %bitcast.96, bf16[256,4096]{1,0:T(8,128)(2,1)S(1)} %copy-done), kind=kOutput, calls=%fused_computation.26 | convolution fusion | flops 2155872256 | bytes 27787264 | tf_op jit(solution)/shard_map/dot_general | solution.py:183
  243.2 197.5 %reduce-scatter.4.cloned.1.call-done = bf16[1024,256]{1,0:T(8,128)(2,1)} async-done(((bf16[1024,4096]{1,0:T(8,128)(2,1)}), bf16[1024,256]{1,0:T(8,128)(2,1)}) %reduce-scatter.4.cloned.1.call-update) | async-done | bytes 524304 | tf_op jit(solution)/shard_map/reduce_scatter | solution.py:187
  440.7 0.3 reduce-scatter.6.cloned.1.call-start
  441.0 0.1 reshape.314
  441.1 77.8 %all-gather.14.cloned.1.call-done = bf16[1024,4096]{1,0:T(8,128)(2,1)} async-done(((bf16[1024,256]{1,0:T(8,128)(2,1)}), bf16[1024,4096]{1,0:T(8,128)(2,1)}) %all-gather.14.cloned.1.call-update) | async-done | bytes 8388624 | tf_op jit(solution)/shard_map/all_gather | solution.py:191
  518.8 5.9 fusion.30
  524.7 0.2 multiply_reduce_fusion
  525.0 4.6 multiply_multiply_fusion
  529.6 9.0 %fusion.32 = f32[16,1024,128]{2,1,0:T(8,128)} fusion(f32[16,64,1024]{2,1,0:T(8,128)S(1)} %multiply_multiply_fusion, bf16[16,64,128]{2,1,0:T(8,128)(2,1)S(1)} %bitcast.104), kind=kOutput, calls=%fused_computation.63 | convolution fusion | flops 1610612736 | bytes 12845056 | tf_op jit(solution)/shard_map/bhqk,bqhd->bkhd/dot_general | solution.py:66
  538.5 2.5 broadcast.200.clone
  541.0 39.0 %scatter_fusion = f32[128,64,128]{2,1,0:T(8,128)} fusion(f32[128,64,128]{2,1,0:T(8,128)} %broadcast.200.clone, s32[256]{0:T(256)S(1)} %bitcast.106, f32[256,64,128]{2,1,0:T(8,128)} %bitcast.85), kind=kCustom, calls=%fused_computation.4 | custom fusion | flops 2097152 | bytes 25166848 | tf_op jit(solution)/shard_map/scatter-add | solution.py:77
  580.1 4.0 convert_element_type.63
  584.1 0.3 reduce-scatter.8.cloned.1.call-start
  584.4 10.6 %convolution_bitcast_fusion = f32[16,1024,1,128]{1,3,0,2:T(8,128)} fusion(f32[16,64,128]{2,1,0:T(8,128)S(1)} %bitcast.101, f32[16,64,1024]{2,1,0:T(8,128)} %get-tuple-element.409, f32[16,64]{1,0:T(8,128)S(1)} %get-tuple-element.408), kind=kOutput, calls=%fused_computation.31 | convolution fusion | flops 1611661312 | bytes 13111296 | tf_op jit(solution)/shard_map/bhqk,bqhd->bkhd/dot_general | solution.py:52
  595.0 9.3 %copy.32 = f32[16,1024,1,128]{3,1,0,2:T(8,128)} copy(f32[16,1024,1,128]{1,3,0,2:T(8,128)} %convolution_bitcast_fusion) | data formatting | bytes 16777216 | tf_op jit(solution)/shard_map/bhqk,bqhd->bkhd/transpose | solution.py:52
  604.3 2.5 broadcast.200.clone.1
  606.8 39.1 %scatter_fusion.1 = f32[128,64,128]{2,1,0:T(8,128)} fusion(f32[128,64,128]{2,1,0:T(8,128)} %broadcast.200.clone.1, s32[256]{0:T(256)S(1)} %bitcast.107, f32[256,64,128]{2,1,0:T(8,128)} %bitcast.84), kind=kCustom, calls=%fused_computation.5 | custom fusion | flops 2097152 | bytes 25166848 | tf_op jit(solution)/shard_map/scatter-add | solution.py:82
  645.9 4.1 convert_element_type.66
  650.0 1.0 convert_element_type.62
  651.1 6.4 fusion.31
  657.5 1.8 convert_element_type.65
  659.2 31.6 %reduce-scatter.8.cloned.1.call-done = bf16[1024,128]{1,0:T(8,128)(2,1)} async-done(((bf16[8192,128]{1,0:T(8,128)(2,1)}), bf16[1024,128]{1,0:T(8,128)(2,1)}) %reduce-scatter.8.cloned.1.call-update) | async-done | bytes 262160 | tf_op jit(solution)/shard_map/reduce_scatter | solution.py:201
  690.8 1.8 convert_element_type.68
  (133 shorter events, 1.4 us)
Async XLA Ops:
  7.2 224.5 %copy-start = (bf16[256,4096]{1,0:T(8,128)(2,1)S(1)}, bf16[256,4096]{1,0:T(8,128)(2,1)}, u32[]{:S(2)}) copy-start(bf16[256,4096]{1,0:T(8,128)(2,1)} %param.17) | copy-start | bytes 6291460
  7.2 6.9 copy-start.12
  7.2 133.8 %all-gather.6.cloned.1.call-start = ((), (), s32[]{:S(2)}) async-start(), calls=%async_computation.3 | async-start | bytes 2359296 | tf_op jit(solution)/shard_map/all_gather | solution.py:170
  7.9 137.8 %all-gather.8.cloned.1.call-start = ((), (), s32[]{:S(2)}) async-start(), calls=%async_computation.4 | async-start | bytes 2359296 | tf_op jit(solution)/shard_map/all_gather | solution.py:169
  8.7 162.7 %all-gather.10.cloned.1.call-start = ((), (), s32[]{:S(2)}) async-start(), calls=%async_computation.5 | async-start | bytes 4718592 | tf_op jit(solution)/shard_map/all_gather | solution.py:161
  10.8 193.1 %all-gather.12.cloned.1.call-start = ((), (), s32[]{:S(2)}) async-start(), calls=%async_computation.6 | async-start | bytes 4718592 | tf_op jit(solution)/shard_map/all_gather | solution.py:162
  12.9 427.8 %reduce-scatter.4.cloned.1.call-start = ((), (), s32[]{:S(2)}) async-start(), calls=%async_computation.7 | async-start | bytes 8912896 | tf_op jit(solution)/shard_map/reduce_scatter | solution.py:187
  49.2 91.2 %copy-start.9 = (bf16[1024,256]{1,0:T(8,128)(2,1)S(1)}, bf16[1024,256]{1,0:T(8,128)(2,1)}, u32[]{:S(2)}) copy-start(bf16[1024,256]{1,0:T(8,128)(2,1)} %param.14) | copy-start | bytes 1572868
  145.8 4.7 copy-start.11
  156.7 6.7 copy-start.7
  207.2 2.3 copy-start.4
  211.5 1.0 copy-start.5
  214.8 2.3 copy-start.4
  219.1 1.0 copy-start.5
  243.1 197.8 %copy-start.13 = (s32[16,16]{1,0:T(8,128)S(1)}, s32[16,16]{1,0:T(8,128)}, u32[]{:S(2)}) copy-start(s32[16,16]{1,0:T(8,128)} %param.23) | copy-start | bytes 3076
  243.1 275.7 %copy-start.8 = (bf16[128,4096]{1,0:T(8,128)(2,1)S(1)}, bf16[128,4096]{1,0:T(8,128)(2,1)}, u32[]{:S(2)}) copy-start(bf16[128,4096]{1,0:T(8,128)(2,1)} %param.21) | copy-start | bytes 3145732
  243.1 275.7 %all-gather.14.cloned.1.call-start = ((), (), s32[]{:S(2)}) async-start(), calls=%async_computation.8 | async-start | bytes 8912896 | tf_op jit(solution)/shard_map/all_gather | solution.py:191
  440.7 216.8 %reduce-scatter.6.cloned.1.call-start = ((), (), s32[]{:S(2)}) async-start(), calls=%async_computation.9 | async-start | bytes 2359296 | tf_op jit(solution)/shard_map/reduce_scatter | solution.py:198
  441.1 83.7 %copy-start.10 = (f32[16,64,1,128]{3,1,0,2:T(8,128)S(1)}, f32[16,64,1,128]{3,1,0,2:T(8,128)}, u32[]{:S(2)}) copy-start(f32[16,64,1,128]{3,1,0,2:T(8,128)} %get-tuple-element.411) | copy-start | bytes 1572868
  518.8 6.1 copy-start.3
  518.8 6.1 copy-start.14
  529.6 9.0 %copy-start.2 = (f32[16,64,1024]{2,1,0:T(8,128)}, f32[16,64,1024]{2,1,0:T(8,128)S(1)}, u32[]{:S(2)}) copy-start(f32[16,64,1024]{2,1,0:T(8,128)S(1)} %multiply_multiply_fusion) | copy-start | bytes 12582916
  584.1 106.7 %reduce-scatter.8.cloned.1.call-start = ((), (), s32[]{:S(2)}) async-start(), calls=%async_computation.10 | async-start | bytes 2359296 | tf_op jit(solution)/shard_map/reduce_scatter | solution.py:201
  645.9 4.1 copy-start.6
  650.0 42.6 %copy-start.1 = (bf16[256,4096]{1,0:T(8,128)(2,1)S(1)}, bf16[256,4096]{1,0:T(8,128)(2,1)}, u32[]{:S(2)}) copy-start(bf16[256,4096]{1,0:T(8,128)(2,1)} %param.17) | copy-start | bytes 6291460
Sparse Core Ops, SparseCore 0:
  9.7 44.3 all-gather.5
  55.7 40.3 all-gather.7
  98.3 52.0 all-gather.9
  152.4 51.3 all-gather.11
  243.3 197.3 reduce-scatter.3
  442.8 76.0 all-gather.13
  584.2 40.2 reduce-scatter.5
  650.1 40.6 reduce-scatter.7
where the time goes:
time: 701 us; the launch traced here: 699 us
  waiting for transfers between devices  341 us (49%)
  local copies, waits for them, and re-layouts  133 us (19%)
  other arithmetic  95.2 us (14%)
  matrix products  74.9 us (11%)
  blocking collectives  28.7 us (4%)
  between operations  14.4 us (2%)
  loops' own time  11.3 us (2%)
    reduce_scatter x1, waiting for transfers between devices, on_device(): lax.psum_scatter(partial_terms.astype(jnp.bfloat16), ('head', 'grp'), sca...  197 us
    gather x2, local copies, waits for them, and re-layouts, student_forward(): key_seg = segment_all[key_pos]  90.6 us
    all_gather x1, waiting for transfers between devices, on_device(): lax.all_gather(mismatch.astype(jnp.bfloat16), ('head', 'grp'), axis=1, ti...  77.8 us
    scatter-add x1, other arithmetic, student_backward(): value_total = jnp.zeros((token_count // BS, BS, width), jnp.float32).at[f...  39.1 us
    scatter-add x1, other arithmetic, student_backward(): key_total = jnp.zeros((token_count // BS, BS, width), jnp.float32).at[fla...  39 us
    all_gather x1, waiting for transfers between devices, on_device(): lax.all_gather(t_value, 'blk', axis=0, tiled=True)  32.4 us
    reduce_scatter x1, waiting for transfers between devices, on_device(): lax.psum_scatter(grad_values.astype(jnp.bfloat16), 'blk', scatter_dimensi...  31.6 us
    all_gather x1, blocking collectives, on_device(): lax.all_gather(segments, 'blk', axis=0, tiled=True)  28.7 us
  transfers between devices with their start and end apart: 8, of which 4 were waited for; matrix products, arithmetic and copies ran while one was open for 30% of the time, Pallas kernels for 0%

commit v1 on v0

--- a/solution.py
+++ b/solution.py
@@ -188,7 +188,15 @@
         partial_terms.astype(jnp.bfloat16), ("head", "grp"), scatter_dimension=1, tiled=True
     ).astype(jnp.float32)
     grad_attn = lax.dot_general(
-        lax.all_gather(mismatch.astype(jnp.bfloat16), ("head", "grp"), axis=1, tiled=True),
+        jnp.concatenate(
+            lax.all_to_all(
+                jnp.stack([mismatch.astype(jnp.bfloat16)] * lax.axis_size(("head", "grp"))),
+                ("head", "grp"),
+                0,
+                0,
+            ),
+            axis=1,
+        ),
         s_out,
         contract,
         preferred_element_type=jnp.float32,

time: 701 us -> 763 us (1.088); the launches traced: 699 us -> 753 us
  local copies, waits for them, and re-layouts: 133 us -> 164 us
  waiting for transfers between devices: 341 us -> 359 us
    all_to_all x0 -> x1, waiting for transfers between devices: none -> 95.3 us  [on_device(): lax.all_to_all(jnp.stack([mismatch.astype(jnp.bfloat16)] * lax.axis_size(...]
    all_gather x1 -> x0, waiting for transfers between devices: 77.8 us -> none  [on_device(): lax.all_gather(mismatch.astype(jnp.bfloat16), ('head', 'grp'), axis=1, ti...]
    dot_general x0 -> x1, local copies, waits for them, and re-layouts: none -> 13.8 us  [on_device(): lax.dot_general(jnp.concatenate(lax.all_to_all(jnp.stack([mismatch.astype...]
    reshape x0 -> x1, local copies, waits for them, and re-layouts: none -> 11.4 us  [on_device(): jnp.concatenate(lax.all_to_all(jnp.stack([mismatch.astype(jnp.bfloat16)]...]
  transfers between devices with their start and end apart: 8 -> 8, of which waited for: 4 -> 4; matrix products, arithmetic and copies ran while one was open for 30% -> 28% of each run, Pallas kernels for 0% -> 0%
where the time goes in v1:
time: 763 us; the launch traced here: 753 us
  waiting for transfers between devices  359 us (47%)
  local copies, waits for them, and re-layouts  164 us (21%)
  other arithmetic  95 us (12%)
  matrix products  75.3 us (10%)
  blocking collectives  28.7 us (4%)
  between operations  14.6 us (2%)
  loops' own time  11.7 us (2%)
    reduce_scatter x1, waiting for transfers between devices, on_device(): lax.psum_scatter(partial_terms.astype(jnp.bfloat16), ('head', 'grp'), sca...  198 us
    all_to_all x1, waiting for transfers between devices, on_device(): lax.all_to_all(jnp.stack([mismatch.astype(jnp.bfloat16)] * lax.axis_size(...  95.3 us
    gather x2, local copies, waits for them, and re-layouts, student_forward(): key_seg = segment_all[key_pos]  90.6 us
    scatter-add x1, other arithmetic, student_backward(): value_total = jnp.zeros((token_count // BS, BS, width), jnp.float32).at[f...  39.1 us
    scatter-add x1, other arithmetic, student_backward(): key_total = jnp.zeros((token_count // BS, BS, width), jnp.float32).at[fla...  39 us
    reduce_scatter x1, waiting for transfers between devices, on_device(): lax.psum_scatter(grad_values.astype(jnp.bfloat16), 'blk', scatter_dimensi...  32.5 us
    all_gather x1, waiting for transfers between devices, on_device(): lax.all_gather(t_value, 'blk', axis=0, tiled=True)  32.4 us
    all_gather x1, blocking collectives, on_device(): lax.all_gather(segments, 'blk', axis=0, tiled=True)  28.7 us
  transfers between devices with their start and end apart: 8, of which 4 were waited for; matrix products, arithmetic and copies ran while one was open for 28% of the time, Pallas kernels for 0%

profile of v1, /device:TPU:0, one launch (start us, length us, event | category | flops | bytes accessed | tf_op | source)
XLA Modules:
  0.0 753.3 jit_solution(7252078792190482699)
XLA Ops:
  7.2 0.7 all-gather.5.cloned.1.call-update
  8.0 0.7 all-gather.7.cloned.1.call-update
  8.7 2.0 copy.27
  10.8 2.0 copy.29
  13.0 0.7 broadcast_multiply_fusion
  13.7 0.1 add.182
  13.8 0.1 add.190
  13.9 0.1 add.183
  14.0 0.1 reshape.328
  14.1 28.7 %all_gather.17 = s32[8192]{0:T(1024)S(1)} all-gather(s32[1024]{0:T(1024)S(1)} %copy-done.11), channel_id=1, replica_groups=mesh['blk'=8,'head'=8,'grp'=2] {'blk'}, dimensions={0}, use_global_device_ids=true | all-gather | bytes 36864 | tf_op jit(solution)/shard_map/all_gather | solution.py:171
  42.8 6.1 gather_fusion.2
  49.2 90.5 %gather_fusion.1 = s32[16384]{0:T(1024)S(1)} fusion(s32[8192]{0:T(1024)S(1)} %all_gather.17, s32[16384]{0:T(1024)S(1)} %broadcast_clamp_fusion), kind=kCustom, calls=%fused_computation.1 | custom fusion | bytes 196608 | tf_op jit(solution)/shard_map/gather | solution.py:28
  139.8 0.6 slice.3
  140.4 0.2 copy.28
  140.6 0.3 copy.30
  141.0 4.8 gather_fusion
  145.8 4.7 gather_fusion.3
  150.5 6.2 fusion.30
  156.7 6.7 fusion.31
  163.3 8.1 %fusion.32 = f32[1024,4096]{1,0:T(8,128)} fusion(bf16[1024,128]{1,0:T(8,128)(2,1)S(1)} %bitcast.106, bf16[128,4096]{1,0:T(8,128)(2,1)S(1)} %copy-done.7), kind=kOutput, calls=%fused_computation.63 | convolution fusion | flops 1073741824 | bytes 18087936 | tf_op jit(solution)/shard_map/dot_general | solution.py:183
  171.4 32.4 %all-gather.11.cloned.1.call-done = bf16[8192,256]{0,1:T(8,128)(2,1)} async-done(((bf16[1024,256]{0,1:T(8,128)(2,1)}), bf16[8192,256]{0,1:T(8,128)(2,1)}) %all-gather.11.cloned.1.call-update) | async-done | bytes 4194320 | tf_op jit(solution)/shard_map/all_gather | solution.py:162
  203.9 1.0 broadcast_in_dim.72
  204.9 25.6 %while.18 = (s32[]{:T(128)}, f32[2,1024]{1,0:T(2,128)S(1)}, f32[2,1024]{1,0:T(2,128)S(1)}, f32[2,1024,128]{2,1,0:T(8,128)}, s32[]{:T(128)}, /*index=5*/s32[8192]...) while((s32[]{:T(128)}, f32[2,1024]{1,0:T(2,128)S(1)}, ...), condition=%wide.region_7.8_spmd.clone, body=%wide.region_2.7_spmd.clone.sunk | while | flops 552605184 | bytes 27425168 | solution.py:142
  206.0 7.0 conditional.3
  206.0 0.1 dynamic_slice.34
  206.1 0.5 compare_and_fusion
  206.6 1.1 constant_dynamic-slice_fusion
  207.7 1.1 fusion.2
  208.8 1.1 fusion.4
  210.0 2.0 fusion.8
  212.0 1.0 copy-done.5
  213.6 7.0 conditional.3
  213.7 0.5 compare_and_fusion
  214.2 1.1 constant_dynamic-slice_fusion
  215.3 1.1 fusion.2
  216.4 1.1 fusion.4
  217.6 2.0 fusion.8
  219.6 1.0 copy-done.5
  230.5 1.6 copy.31
  232.0 0.1 divide_convert_fusion
  232.2 11.4 %subtract_convert_fusion = bf16[1024,4096]{1,0:T(8,128)(2,1)} fusion(f32[1024,4096]{1,0:T(8,128)} %fusion.32, bf16[1024,256]{0,1:T(8,128)(2,1)S(1)} %bitcast.103, bf16[256,4096]{1,0:T(8,128)(2,1)S(1)} %copy-done), kind=kOutput, calls=%fused_computation.26 | convolution fusion | flops 2155872256 | bytes 27787264 | tf_op jit(solution)/shard_map/dot_general | solution.py:183
  243.6 197.5 %reduce-scatter.4.cloned.1.call-done = bf16[1024,256]{1,0:T(8,128)(2,1)} async-done(((bf16[1024,4096]{1,0:T(8,128)(2,1)}), bf16[1024,256]{1,0:T(8,128)(2,1)}) %reduce-scatter.4.cloned.1.call-update) | async-done | bytes 524304 | tf_op jit(solution)/shard_map/reduce_scatter | solution.py:187
  441.1 5.1 stack.2
  446.2 4.9 all-to-all-start
  451.1 0.1 reshape.321
  451.2 95.3 %all-to-all-done = bf16[16,1024,256]{2,1,0:T(8,128)(2,1)} async-done(((bf16[16,1024,256]{2,1,0:T(8,128)(2,1)}), bf16[16,1024,256]{2,1,0:T(8,128)(2,1)}, u32[]{:S(2)}, u32[]{:S(2)}) %all-to-all-start) | async-done | bytes 8388640 | tf_op jit(solution)/shard_map/all_to_all | solution.py:192
  546.5 11.4 %copy.32 = bf16[1024,16,256]{2,1,0:T(8,128)(2,1)} copy(bf16[1024,16,256]{2,0,1:T(8,128)(2,1)} %bitcast.16) | data formatting | bytes 16777216 | tf_op jit(solution)/shard_map/reshape | solution.py:191
  557.9 13.8 %dot_general.56 = bf16[16,64,4096]{2,1,0:T(8,128)(2,1)} reshape(bf16[1024,16,256]{2,1,0:T(8,128)(2,1)} %copy.32) | data formatting | bytes 16777216 | tf_op jit(solution)/shard_map/dot_general | solution.py:190
  571.7 5.9 fusion.24
  577.7 4.6 multiply_multiply_fusion
  582.3 9.0 %fusion.34 = f32[16,1024,128]{2,1,0:T(8,128)} fusion(f32[16,64,1024]{2,1,0:T(8,128)S(1)} %multiply_multiply_fusion, bf16[16,64,128]{2,1,0:T(8,128)(2,1)S(1)} %bitcast.108), kind=kOutput, calls=%fused_computation.65 | convolution fusion | flops 1610612736 | bytes 12845056 | tf_op jit(solution)/shard_map/bhqk,bqhd->bkhd/dot_general | solution.py:66
  591.2 2.5 broadcast.202.clone
  593.8 39.0 %scatter_fusion = f32[128,64,128]{2,1,0:T(8,128)} fusion(f32[128,64,128]{2,1,0:T(8,128)} %broadcast.202.clone, s32[256]{0:T(256)S(1)} %bitcast.110, f32[256,64,128]{2,1,0:T(8,128)} %bitcast.92), kind=kCustom, calls=%fused_computation.4 | custom fusion | flops 2097152 | bytes 25166848 | tf_op jit(solution)/shard_map/scatter-add | solution.py:77
  632.8 4.0 convert_element_type.63
  636.9 10.8 %convolution_bitcast_fusion = f32[16,1024,1,128]{1,3,0,2:T(8,128)} fusion(f32[16,64,128]{2,1,0:T(8,128)S(1)} %get-tuple-element.413, f32[16,64,1024]{2,1,0:T(8,128)} %get-tuple-element.409, f32[16,64]{1,0:T(8,128)S(1)} %get-tuple-element.408), kind=kOutput, calls=%fused_computation.31 | convolution fusion | flops 1611661312 | bytes 13111296 | tf_op jit(solution)/shard_map/bhqk,bqhd->bkhd/dot_general | solution.py:52
  647.7 9.3 %copy.33 = f32[16,1024,1,128]{3,1,0,2:T(8,128)} copy(f32[16,1024,1,128]{1,3,0,2:T(8,128)} %convolution_bitcast_fusion) | data formatting | bytes 16777216 | tf_op jit(solution)/shard_map/bhqk,bqhd->bkhd/transpose | solution.py:52
  657.0 2.5 broadcast.202.clone.1
  659.5 39.1 %scatter_fusion.1 = f32[128,64,128]{2,1,0:T(8,128)} fusion(f32[128,64,128]{2,1,0:T(8,128)} %broadcast.202.clone.1, s32[256]{0:T(256)S(1)} %bitcast.111, f32[256,64,128]{2,1,0:T(8,128)} %bitcast.91), kind=kCustom, calls=%fused_computation.5 | custom fusion | flops 2097152 | bytes 25166848 | tf_op jit(solution)/shard_map/scatter-add | solution.py:82
  698.6 4.1 convert_element_type.66
  702.7 1.0 convert_element_type.62
  703.8 6.4 fusion.33
  710.2 1.8 convert_element_type.65
  712.0 32.5 %reduce-scatter.8.cloned.1.call-done = bf16[1024,128]{1,0:T(8,128)(2,1)} async-done(((bf16[8192,128]{1,0:T(8,128)(2,1)}), bf16[1024,128]{1,0:T(8,128)(2,1)}) %reduce-scatter.8.cloned.1.call-update) | async-done | bytes 262160 | tf_op jit(solution)/shard_map/reduce_scatter | solution.py:209
  744.4 1.8 convert_element_type.68
  (134 shorter events, 1.5 us)
Async XLA Ops:
  7.2 225.0 %copy-start = (bf16[256,4096]{1,0:T(8,128)(2,1)S(1)}, bf16[256,4096]{1,0:T(8,128)(2,1)}, u32[]{:S(2)}) copy-start(bf16[256,4096]{1,0:T(8,128)(2,1)} %param.17) | copy-start | bytes 6291460
  7.2 6.9 copy-start.11
  7.2 133.8 %all-gather.5.cloned.1.call-start = ((), (), s32[]{:S(2)}) async-start(), calls=%async_computation.4 | async-start | bytes 2359296 | tf_op jit(solution)/shard_map/all_gather | solution.py:170
  7.9 137.8 %all-gather.7.cloned.1.call-start = ((), (), s32[]{:S(2)}) async-start(), calls=%async_computation.5 | async-start | bytes 2359296 | tf_op jit(solution)/shard_map/all_gather | solution.py:169
  8.7 162.7 %all-gather.9.cloned.1.call-start = ((), (), s32[]{:S(2)}) async-start(), calls=%async_computation.6 | async-start | bytes 4718592 | tf_op jit(solution)/shard_map/all_gather | solution.py:161
  10.8 193.1 %all-gather.11.cloned.1.call-start = ((), (), s32[]{:S(2)}) async-start(), calls=%async_computation.7 | async-start | bytes 4718592 | tf_op jit(solution)/shard_map/all_gather | solution.py:162
  12.9 428.2 %reduce-scatter.4.cloned.1.call-start = ((), (), s32[]{:S(2)}) async-start(), calls=%async_computation.8 | async-start | bytes 8912896 | tf_op jit(solution)/shard_map/reduce_scatter | solution.py:187
  49.2 91.2 %copy-start.9 = (bf16[1024,256]{1,0:T(8,128)(2,1)S(1)}, bf16[1024,256]{1,0:T(8,128)(2,1)}, u32[]{:S(2)}) copy-start(bf16[1024,256]{1,0:T(8,128)(2,1)} %param.14) | copy-start | bytes 1572868
  145.8 4.7 copy-start.10
  156.7 6.7 copy-start.7
  207.7 2.3 copy-start.4
  212.0 1.0 copy-start.5
  215.3 2.3 copy-start.4
  219.6 1.0 copy-start.5
  446.2 4.9 copy-start.12
  446.2 100.3 %all-to-all-start = ((bf16[16,1024,256]{2,1,0:T(8,128)(2,1)}), bf16[16,1024,256]{2,1,0:T(8,128)(2,1)}, u32[]{:S(2)}, u32[]{:S(2)}) async-start(bf16[16,1024,256]{2,1,0:T(8,128)(2,1)} %stack.2), calls=%async_computation.1 | async-start | bytes 16777216 | tf_op jit(solution)/shard_map/all_to_all | solution.py:192
  451.1 259.1 %reduce-scatter.6.cloned.1.call-start = ((), (), s32[]{:S(2)}) async-start(), calls=%async_computation.9 | async-start | bytes 2359296 | tf_op jit(solution)/shard_map/reduce_scatter | solution.py:206
  557.9 13.8 %copy-start.8 = (bf16[128,4096]{1,0:T(8,128)(2,1)S(1)}, bf16[128,4096]{1,0:T(8,128)(2,1)}, u32[]{:S(2)}) copy-start(bf16[128,4096]{1,0:T(8,128)(2,1)} %param.21) | copy-start | bytes 3145732
  557.9 13.8 %copy-start.14 = (f32[16,64,1,128]{3,1,0,2:T(8,128)S(1)}, f32[16,64,1,128]{3,1,0,2:T(8,128)}, u32[]{:S(2)}) copy-start(f32[16,64,1,128]{3,1,0,2:T(8,128)} %get-tuple-element.411) | copy-start | bytes 1572868
  571.7 6.0 copy-start.3
  571.7 6.0 copy-start.13
  582.3 9.0 %copy-start.2 = (f32[16,64,1024]{2,1,0:T(8,128)}, f32[16,64,1024]{2,1,0:T(8,128)S(1)}, u32[]{:S(2)}) copy-start(f32[16,64,1024]{2,1,0:T(8,128)S(1)} %multiply_multiply_fusion) | copy-start | bytes 12582916
  636.8 107.6 %reduce-scatter.8.cloned.1.call-start = ((), (), s32[]{:S(2)}) async-start(), calls=%async_computation.10 | async-start | bytes 2359296 | tf_op jit(solution)/shard_map/reduce_scatter | solution.py:209
  698.6 4.1 copy-start.6
  702.7 43.5 %copy-start.1 = (bf16[256,4096]{1,0:T(8,128)(2,1)S(1)}, bf16[256,4096]{1,0:T(8,128)(2,1)}, u32[]{:S(2)}) copy-start(bf16[256,4096]{1,0:T(8,128)(2,1)} %param.17) | copy-start | bytes 6291460
Sparse Core Ops, SparseCore 0:
  9.7 44.3 all-gather.4
  55.7 40.3 all-gather.6
  98.3 52.0 all-gather.8
  152.4 51.3 all-gather.10
  243.7 197.3 reduce-scatter.3
  636.9 41.3 reduce-scatter.5
  702.8 41.5 reduce-scatter.7
